TPU v7x, 256 devices: a whole 4x4x8 slice. The times are simulated.
256 devices in a mesh: obs: 64 (over z, x, core), sub: 4 (over y).
Axes of the slice: x: 4, y: 4, z: 8, core: 2. Of those that a mesh axis runs over, the one named last changes fastest.
Arguments:
- jacobian: bfloat16 [262144, 2048], P(('obs', 'sub')), may hold values from -0.09375 to 0.09375
- obs_weight: float32 [262144], P(('obs', 'sub')), may hold values from 0.2 to 5
- row_counts: int32 [64], P('obs'), may hold values from 1 to 4096, 196608 in all
- tile_lists: int32 [64, 8], replicated, may hold values from 0 to 15, all different within a row
- tile_slot: int32 [16], replicated, may hold values from 0 to 15, each once
- probe_block: bfloat16 [4096, 256], P('obs'), may hold values from -6 to 6
Outputs:
- owned_product: bfloat16 [4096, 256], P('obs', 'sub')
Inputs may be any that keep to these rules, and one draw needn't show every extreme that they name: `row_counts`: the live counts of one block; some block is full (4096) in every draw. `tile_lists`: each row lists 8 different tiles; every tile is listed by some block. `tile_slot`: a permutation of the tiles.
All inputs are finite; a program needn't handle non-finite values.
Results may differ from a plain program's by a relative error of at most 0.0034.
Values may be sent and summed in bfloat16 or wider, within the bound.
A program may use at most 64 MiB of HBM per device.

v0:
```python
import jax
import jax.numpy as jnp
from jax import lax
from jax.sharding import PartitionSpec as P


def local(jacobian, obs_weight, row_counts, tile_lists, tile_slot, probe_block):
    rows = jacobian.shape[0]
    width = jacobian.shape[1]
    tiles_listed = tile_lists.shape[1]
    tile_count = tile_slot.shape[0]
    tile_rows = width // tiles_listed
    obs_count = lax.axis_size("obs")
    own_rows = tile_count * tile_rows // obs_count
    block_id = lax.axis_index("obs")
    sub_id = lax.axis_index("sub")
    offset = sub_id * rows
    live = (offset + jnp.arange(rows, dtype=jnp.int32) < row_counts[0]).astype(jnp.float32)
    weighted = (jacobian.astype(jnp.float32) * (obs_weight * live)[:, None]).astype(jnp.bfloat16)
    my_tiles = lax.dynamic_slice_in_dim(tile_lists, block_id, 1, 0)[0]
    contract_rows = (((0,), (0,)), ((), ()))
    within = jnp.arange(tile_rows, dtype=jnp.int32)
    wanted_rows = (my_tiles[:, None] * tile_rows + within[None, :]).reshape(width)
    piece = lax.all_gather(probe_block, "obs", axis=0, tiled=True)
    global_rows = jnp.arange(piece.shape[0], dtype=jnp.int32)
    selector = (wanted_rows[:, None] == global_rows[None, :]).astype(jnp.bfloat16)
    probe_cols = jnp.dot(selector, piece, preferred_element_type=jnp.float32).astype(jnp.bfloat16)
    image = jnp.dot(jacobian, probe_cols, preferred_element_type=jnp.float32).astype(jnp.bfloat16)
    partial_prod = lax.dot_general(
        weighted, image, contract_rows, preferred_element_type=jnp.float32
    )
    tile_ids = jnp.arange(tile_count, dtype=jnp.int32)
    slots = jnp.sum(
        (my_tiles[:, None] == tile_ids[None, :]).astype(jnp.int32) * tile_slot[None, :], axis=1
    )
    positions = jnp.arange(tiles_listed, dtype=jnp.int32)
    block_sum = lax.psum_scatter(partial_prod, "sub", scatter_dimension=1, tiled=True)
    targets = jnp.arange(own_rows * lax.axis_size("obs"), dtype=jnp.int32)
    target_slot = targets // tile_rows
    match = (slots[None, :] == target_slot[:, None]).astype(jnp.int32)
    found = jnp.sum(match, axis=1)
    where_at = jnp.sum(match * positions[None, :], axis=1)
    source_rows = where_at * tile_rows + targets % tile_rows
    taken = jnp.take(block_sum, source_rows, axis=0)
    summed = lax.psum_scatter(
        taken * found[:, None].astype(jnp.float32), "obs", scatter_dimension=0, tiled=True
    )
    return summed.astype(jnp.bfloat16)


def solution(mesh):
    placed = (P(("obs", "sub"), None), P(("obs", "sub")), P("obs"), P(), P(), P("obs", None))
    return jax.shard_map(
        local, mesh=mesh, in_specs=placed, out_specs=P("obs", "sub"), check_vma=False
    )
```

profile of v0, /device:TPU:8, one launch (start us, length us, event | category | flops | bytes accessed | tf_op | source)
XLA Modules:
  0.0 300.9 jit_solution(16359943806372789093)
XLA Ops:
  6.5 0.0 copy-start
  6.5 0.0 all-gather.2.cloned.1.call-start
  6.5 0.7 all-gather.2.cloned.1.call-update
  7.3 0.0 reduce-scatter.3.cloned.1.call-start
  8.0 0.0 copy-done
  8.0 0.2 dynamic-slice_reduce_fusion
  8.2 0.1 add_bitcast_fusion
  8.2 0.7 fusion.18
  8.9 81.4 %all-gather.2.cloned.1.call-done = bf16[4096,256]{1,0:T(8,128)(2,1)} async-done(((bf16[64,256]{1,0:T(8,128)(2,1)}), bf16[4096,256]{1,0:T(8,128)(2,1)}) %all-gather.2.cloned.1.call-update) | async-done | bytes 2097168 | tf_op jit(solution)/shard_map/all_gather | solution.py:24
  90.3 11.4 %fusion.6 = bf16[256,1024]{1,0:T(8,128)(2,1)S(1)} fusion(bf16[1024,2048]{1,0:T(8,128)(2,1)} %param.6, bf16[4096,256]{1,0:T(8,128)(2,1)} %all-gather.2.cloned.1.call-done, s32[2048]{0:T(1024)S(1)} %bitcast.12), kind=kOutput, calls=%fused_computation.10 | convolution fusion | flops 5377884160 | bytes 6823936 | tf_op jit(solution)/shard_map/dot_general | solution.py:28
  101.7 4.9 %fusion.2 = f32[2048,256]{0,1:T(8,128)} fusion(bf16[256,1024]{1,0:T(8,128)(2,1)S(1)} %fusion.6, bf16[1024,2048]{1,0:T(8,128)(2,1)} %param.6, f32[1024]{0:T(1024)S(1)} %fusion.18), kind=kOutput, calls=%fused_computation.5 | convolution fusion | flops 1080033280 | bytes 6819840 | tf_op jit(solution)/shard_map/dot_general | solution.py:29
  106.6 0.0 copy-start.1
  106.6 0.0 reduce-scatter.3.cloned.1.call-update
  106.7 0.0 reduce-scatter.5.cloned.1.call-start
  106.7 0.6 copy-done.1
  107.3 0.2 select_reduce_fusion
  107.5 0.1 fusion.8
  107.7 27.8 %reduce-scatter.3.cloned.1.call-done = f32[2048,64]{0,1:T(8,128)} async-done(((f32[2048,256]{0,1:T(8,128)}), f32[2048,64]{0,1:T(8,128)}) %reduce-scatter.3.cloned.1.call-update) | async-done | bytes 524304 | tf_op jit(solution)/shard_map/reduce_scatter | solution.py:37
  135.5 1.4 copy.9
  136.9 10.8 %gather_fusion = f32[4096,64]{1,0:T(8,128)S(1)} fusion(f32[2048,64]{1,0:T(8,128)S(1)} %copy.9, s32[4096]{0:T(1024)S(1)} %broadcast_clamp_fusion), kind=kCustom, calls=%fused_computation | custom fusion | bytes 2113536 | tf_op jit(solution)/shard_map/jit(_take)/gather | solution.py:44
  147.6 2.7 select_multiply_fusion
  150.3 0.0 reduce-scatter.5.cloned.1.call-update
  150.3 142.7 %reduce-scatter.5.cloned.1.call-done = f32[64,64]{1,0:T(8,128)} async-done(((f32[4096,64]{1,0:T(8,128)}), f32[64,64]{1,0:T(8,128)}) %reduce-scatter.5.cloned.1.call-update) | async-done | bytes 16400 | tf_op jit(solution)/shard_map/reduce_scatter | solution.py:45
  293.0 1.4 convert_element_type.36
  (8 shorter events, 0.1 us)
Async XLA Ops:
  6.5 1.4 copy-start
  6.5 83.8 %all-gather.2.cloned.1.call-start = ((), (), s32[]{:S(2)}) async-start(), calls=%async_computation.2 | async-start | bytes 2129920 | tf_op jit(solution)/shard_map/all_gather | solution.py:24
  7.3 128.2 %reduce-scatter.3.cloned.1.call-start = ((), (), s32[]{:S(2)}) async-start(), calls=%async_computation.3 | async-start | bytes 2621440 | tf_op jit(solution)/shard_map/reduce_scatter | solution.py:37
  106.6 0.7 copy-start.1
  106.7 186.4 %reduce-scatter.5.cloned.1.call-start = ((), (), s32[]{:S(2)}) async-start(), calls=%async_computation.4 | async-start | bytes 2129920 | tf_op jit(solution)/shard_map/reduce_scatter | solution.py:45
Sparse Core Ops, SparseCore 0:
  10.1 80.1 all-gather.1
  106.8 28.6 reduce-scatter.2
  150.4 142.5 reduce-scatter.4
where the time goes:
time: 301 us
  waiting for transfers between devices  253 us (84%)
  matrix products  16.3 us (5%)
  between operations  13.8 us (5%)
  local copies, waits for them, and re-layouts  12.9 us (4%)
  other arithmetic  5.19 us (2%)
    reduce_scatter x1, waiting for transfers between devices, local(): lax.psum_scatter(taken * found[:, None].astype(jnp.float32), 'obs', scatt...  143 us
    all_gather x1, waiting for transfers between devices, local(): piece = lax.all_gather(probe_block, 'obs', axis=0, tiled=True)  81.4 us
    reduce_scatter x1, waiting for transfers between devices, local(): lax.psum_scatter(partial_prod, 'sub', scatter_dimension=1, tiled=True)  27.8 us
    dot_general x1, matrix products, local(): jnp.dot(jacobian, probe_cols, preferred_element_type=jnp.float32)  11.4 us
    gather x1, local copies, waits for them, and re-layouts, local(): taken = jnp.take(block_sum, source_rows, axis=0)  10.8 us
  transfers between devices with their start and end apart: 3, of which 3 were waited for; matrix products, arithmetic and copies ran while one was open for 0% of the time, Pallas kernels for 0%

commit v1 on v0

--- a/solution.py
+++ b/solution.py
@@ -21,7 +21,9 @@
     contract_rows = (((0,), (0,)), ((), ()))
     within = jnp.arange(tile_rows, dtype=jnp.int32)
     wanted_rows = (my_tiles[:, None] * tile_rows + within[None, :]).reshape(width)
-    piece = lax.all_gather(probe_block, "obs", axis=0, tiled=True)
+    piece = jnp.concatenate(
+        lax.all_to_all(jnp.stack([probe_block] * lax.axis_size("obs")), "obs", 0, 0), axis=0
+    )
     global_rows = jnp.arange(piece.shape[0], dtype=jnp.int32)
     selector = (wanted_rows[:, None] == global_rows[None, :]).astype(jnp.bfloat16)
     probe_cols = jnp.dot(selector, piece, preferred_element_type=jnp.float32).astype(jnp.bfloat16)

time: 301 us -> 282 us (0.937)
  waiting for transfers between devices: 253 us -> 219 us
  starting transfers between devices: 0.08 us -> 12.1 us
    all_gather x1 -> x0, waiting for transfers between devices: 81.4 us -> none  [local(): piece = lax.all_gather(probe_block, 'obs', axis=0, tiled=True)]
    all_to_all x0 -> x1, waiting for transfers between devices: none -> 50.3 us  [local(): lax.all_to_all(jnp.stack([probe_block] * lax.axis_size('obs')), 'obs', 0, 0)]
    all_to_all x0 -> x1, starting transfers between devices: none -> 12.1 us  [local(): lax.all_to_all(jnp.stack([probe_block] * lax.axis_size('obs')), 'obs', 0, 0)]
where the time goes in v1:
time: 282 us; the launch traced here: 281 us
  waiting for transfers between devices  219 us (78%)
  matrix products  15.7 us (6%)
  local copies, waits for them, and re-layouts  15.3 us (5%)
  between operations  14.2 us (5%)
  starting transfers between devices  12.1 us (4%)
  other arithmetic  4.5 us (2%)
    reduce_scatter x1, waiting for transfers between devices, local(): lax.psum_scatter(taken * found[:, None].astype(jnp.float32), 'obs', scatt...  143 us
    all_to_all x1, waiting for transfers between devices, local(): lax.all_to_all(jnp.stack([probe_block] * lax.axis_size('obs')), 'obs', 0, 0)  50.3 us
    reduce_scatter x1, waiting for transfers between devices, local(): lax.psum_scatter(partial_prod, 'sub', scatter_dimension=1, tiled=True)  26.4 us
    all_to_all x1, starting transfers between devices, local(): lax.all_to_all(jnp.stack([probe_block] * lax.axis_size('obs')), 'obs', 0, 0)  12.1 us
    dot_general x1, matrix products, local(): jnp.dot(jacobian, probe_cols, preferred_element_type=jnp.float32)  10.8 us
    gather x1, local copies, waits for them, and re-layouts, local(): taken = jnp.take(block_sum, source_rows, axis=0)  10.8 us
  transfers between devices with their start and end apart: 3, of which 3 were waited for; matrix products, arithmetic and copies ran while one was open for 0% of the time, Pallas kernels for 0%

profile of v1, /device:TPU:8, one launch (start us, length us, event | category | flops | bytes accessed | tf_op | source)
XLA Modules:
  0.0 281.2 jit_solution(925382747368301808)
XLA Ops:
  6.5 0.0 copy-start
  6.5 2.4 stack.2
  8.9 0.0 copy-start.1
  8.9 12.1 %all-to-all-start = ((bf16[64,64,256]{2,1,0:T(8,128)(2,1)}), bf16[64,64,256]{2,1,0:T(8,128)(2,1)S(1)}, u32[]{:S(2)}, u32[]{:S(2)}) async-start(bf16[64,64,256]{2,1,0:T(8,128)(2,1)} %stack.2), calls=%async_computation | async-start | bytes 4194304 | tf_op jit(solution)/shard_map/all_to_all | solution.py:25
  21.0 0.0 reduce-scatter.3.cloned.1.call-start
  21.0 0.0 copy-done
  21.1 0.2 dynamic-slice_reduce_fusion
  21.2 0.1 add_bitcast_fusion
  22.0 0.0 copy-done.1
  22.0 50.3 %all-to-all-done = bf16[64,64,256]{2,1,0:T(8,128)(2,1)S(1)} async-done(((bf16[64,64,256]{2,1,0:T(8,128)(2,1)}), bf16[64,64,256]{2,1,0:T(8,128)(2,1)S(1)}, u32[]{:S(2)}, u32[]{:S(2)}) %all-to-all-start) | async-done | bytes 2097184 | tf_op jit(solution)/shard_map/all_to_all | solution.py:25
  72.3 10.8 %fusion.6 = bf16[256,1024]{1,0:T(8,128)(2,1)S(1)} fusion(bf16[1024,2048]{1,0:T(8,128)(2,1)} %param.6, bf16[4096,256]{1,0:T(8,128)(2,1)S(1)} %bitcast.11, s32[2048]{0:T(1024)S(1)} %bitcast.14), kind=kOutput, calls=%fused_computation.10 | convolution fusion | flops 5377884160 | bytes 6823936 | tf_op jit(solution)/shard_map/dot_general | solution.py:30
  83.1 4.9 %fusion.2 = f32[2048,256]{0,1:T(8,128)} fusion(bf16[256,1024]{1,0:T(8,128)(2,1)S(1)} %fusion.6, bf16[1024,2048]{1,0:T(8,128)(2,1)} %param.6, f32[1024]{0:T(1024)S(1)} %fusion.18), kind=kOutput, calls=%fused_computation.5 | convolution fusion | flops 1080033280 | bytes 6819840 | tf_op jit(solution)/shard_map/dot_general | solution.py:31
  88.0 0.0 copy-start.2
  88.0 0.0 reduce-scatter.3.cloned.1.call-update
  88.1 0.0 reduce-scatter.5.cloned.1.call-start
  88.1 0.6 copy-done.2
  88.7 0.2 select_reduce_fusion
  88.9 0.1 fusion.8
  89.1 26.4 %reduce-scatter.3.cloned.1.call-done = f32[2048,64]{0,1:T(8,128)} async-done(((f32[2048,256]{0,1:T(8,128)}), f32[2048,64]{0,1:T(8,128)}) %reduce-scatter.3.cloned.1.call-update) | async-done | bytes 524304 | tf_op jit(solution)/shard_map/reduce_scatter | solution.py:39
  115.5 1.4 copy.9
  116.9 10.8 %gather_fusion = f32[4096,64]{1,0:T(8,128)S(1)} fusion(f32[2048,64]{1,0:T(8,128)S(1)} %copy.9, s32[4096]{0:T(1024)S(1)} %broadcast_clamp_fusion), kind=kCustom, calls=%fused_computation | custom fusion | bytes 2113536 | tf_op jit(solution)/shard_map/jit(_take)/gather | solution.py:46
  127.7 2.7 select_multiply_fusion
  130.3 0.0 reduce-scatter.5.cloned.1.call-update
  130.3 142.6 %reduce-scatter.5.cloned.1.call-done = f32[64,64]{1,0:T(8,128)} async-done(((f32[4096,64]{1,0:T(8,128)}), f32[64,64]{1,0:T(8,128)}) %reduce-scatter.5.cloned.1.call-update) | async-done | bytes 16400 | tf_op jit(solution)/shard_map/reduce_scatter | solution.py:47
  273.0 1.4 convert_element_type.36
  (9 shorter events, 0.1 us)
Async XLA Ops:
  6.5 14.5 %copy-start = (s32[64,8]{0,1:T(8,128)S(1)}, s32[64,8]{0,1:T(8,128)}, u32[]{:S(2)}) copy-start(s32[64,8]{0,1:T(8,128)} %param.9) | copy-start | bytes 6148
  8.9 13.1 %copy-start.1 = (f32[1024]{0:T(1024)S(1)}, f32[1024]{0:T(1024)}, u32[]{:S(2)}) copy-start(f32[1024]{0:T(1024)} %param.7) | copy-start | bytes 12292
  8.9 63.4 %all-to-all-start = ((bf16[64,64,256]{2,1,0:T(8,128)(2,1)}), bf16[64,64,256]{2,1,0:T(8,128)(2,1)S(1)}, u32[]{:S(2)}, u32[]{:S(2)}) async-start(bf16[64,64,256]{2,1,0:T(8,128)(2,1)} %stack.2), calls=%async_computation | async-start | bytes 4194304 | tf_op jit(solution)/shard_map/all_to_all | solution.py:25
  21.0 94.5 %reduce-scatter.3.cloned.1.call-start = ((), (), s32[]{:S(2)}) async-start(), calls=%async_computation.3 | async-start | bytes 2621440 | tf_op jit(solution)/shard_map/reduce_scatter | solution.py:39
  88.0 0.7 copy-start.2
  88.1 184.9 %reduce-scatter.5.cloned.1.call-start = ((), (), s32[]{:S(2)}) async-start(), calls=%async_computation.4 | async-start | bytes 2129920 | tf_op jit(solution)/shard_map/reduce_scatter | solution.py:47
Sparse Core Ops, SparseCore 0:
  88.2 27.2 reduce-scatter.2
  130.5 142.4 reduce-scatter.4
